TPU v7x, 32 devices: a whole 2x2x4 slice. The times are simulated.
32 devices in a mesh: row: 8 (over y, x, core), col: 4 (over z).
Axes of the slice: x: 2, y: 2, z: 4, core: 2. Of those that a mesh axis runs over, the one named last changes fastest.
Arguments:
- coeffs: bfloat16 [6144, 4096], P('row', 'col'), may hold values from -0.00390625 to 0.00390625
- occupation: float32 [4096], P('col'), may hold values from 0.5 to 2
- basis_on_grid: bfloat16 [320, 512, 512], P('row'), may hold values from -6 to 6
- basis_map: int32 [320, 512], P('row'), may hold values from 0 to 6143, as said below
- basis_count: int32 [320], P('row'), may hold values from 256 to 512
- batch_atom: int32 [320], P('row'), may hold values from 0 to 63
- harmonics: float32 [320, 49, 512], P('row'), may hold values from -0.25 to 0.25
Outputs:
- density: float32 [320, 512], P('row', 'col')
- moments: float32 [64, 49], replicated
Inputs may be any that keep to these rules, and one draw needn't show every extreme that they name: `basis_map`: the slots of one batch name distinct basis functions. With R = 768 and o = b // 40, batch b names only basis functions q * R + (o * 96 + w) mod R with 0 <= q < 8 and 0 <= w < 96.
All inputs are finite; a program needn't handle non-finite values.
Results may differ from a plain program's by a relative error of at most 0.0003.
Values may be sent and summed in bfloat16 or wider, within the bound.
No kernel may reach another device: no remote copies, remote signals or barrier semaphores. Data moves between devices by JAX's collectives and lax.ppermute only.
A program may use at most 192 MiB of HBM per device.

v0:
```python
import jax
import jax.numpy as jnp
from jax import lax
from jax.sharding import PartitionSpec as P

WIN = 96
NATOM = 64


def shards(coeffs, occupation, basis_on_grid, basis_map, basis_count, batch_atom, harmonics):
    batches, points, slots = basis_on_grid.shape
    owned = coeffs.shape[0]
    owners = lax.axis_size("row")
    target = lax.broadcasted_iota(jnp.int32, (owners, WIN), 0)
    offset = lax.broadcasted_iota(jnp.int32, (owners, WIN), 1)
    outgoing_ids = jnp.mod(target * WIN + offset, owned).reshape(-1)
    outgoing = jnp.take(coeffs, outgoing_ids, axis=0)
    window = lax.all_to_all(outgoing, "row", split_axis=0, concat_axis=0, tiled=True)
    start = jnp.mod(lax.axis_index("row") * WIN, owned)
    source = basis_map // owned
    within = jnp.mod(basis_map % owned - start, owned)
    local_ids = source * WIN + within
    selected = jnp.take(window, local_ids, axis=0)
    slot_ids = lax.broadcasted_iota(jnp.int32, (batches, slots), 1)
    keep = slot_ids < basis_count[:, None]
    masked = jnp.where(keep[:, None, :], basis_on_grid, jnp.zeros_like(basis_on_grid))
    orbital = jnp.einsum("bps,bsk->bpk", masked, selected, preferred_element_type=jnp.float32)
    partial_density = jnp.sum(orbital * orbital * occupation[None, None, :], axis=2)
    atom_ids = lax.broadcasted_iota(jnp.int32, (batches, NATOM), 1)
    member = (batch_atom[:, None] == atom_ids).astype(jnp.float32)
    full_density = lax.psum(partial_density, "col")
    local_moment = jnp.einsum(
        "blp,bp->bl", harmonics, full_density, precision=lax.Precision.HIGHEST
    )
    atom_part = jnp.dot(member.T, local_moment, precision=lax.Precision.HIGHEST)
    moments = lax.psum(atom_part, "row")
    share = points // lax.axis_size("col")
    density = lax.dynamic_slice_in_dim(full_density, lax.axis_index("col") * share, share, 1)
    return (density, moments)


def solution(mesh):
    placed = (
        P("row", "col"),
        P("col"),
        P("row", None, None),
        P("row", None),
        P("row"),
        P("row"),
        P("row", None, None),
    )
    return jax.shard_map(
        shards, mesh=mesh, in_specs=placed, out_specs=(P("row", "col"), P()), check_vma=False
    )
```

profile of v0, /device:TPU:0, one launch (start us, length us, event | category | flops | bytes accessed | tf_op | source)
XLA Modules:
  0.0 228.4 jit_solution(9429908495071229577)
XLA Ops:
  7.2 0.0 copy-start
  7.2 0.1 add_remainder_fusion
  7.3 0.1 compare_and_fusion.1
  7.4 0.1 rem.52
  7.5 1.1 copy-done
  8.6 2.8 %gather_fusion = bf16[768,1024]{1,0:T(8,128)(2,1)S(1)} fusion(bf16[768,1024]{1,0:T(8,128)(2,1)S(1)} %copy-done, s32[1024]{0:T(1024)S(1)} %pad_clamp_fusion), kind=kCustom, calls=%fused_computation | custom fusion | bytes 3148800 | tf_op jit(solution)/shard_map/jit(_take)/gather | solution.py:17
  11.4 1.4 broadcast_select_fusion
  12.8 5.2 %all-to-all-start = ((bf16[8,96,1024]{2,1,0:T(8,128)(2,1)}), bf16[8,96,1024]{2,1,0:T(8,128)(2,1)S(1)}, u32[]{:S(2)}, u32[]{:S(2)}) async-start(bf16[8,96,1024]{2,1,0:T(8,128)(2,1)} %broadcast_select_fusion), calls=%async_computation | async-start | bytes 3145728 | tf_op jit(solution)/shard_map/all_to_all | solution.py:18
  18.0 0.0 all-reduce.2.cloned.1.call-start
  18.0 1.0 compare_and_fusion
  19.1 0.7 iota_compare_fusion
  19.9 19.1 %all-to-all-done = bf16[8,96,1024]{2,1,0:T(8,128)(2,1)S(1)} async-done(((bf16[8,96,1024]{2,1,0:T(8,128)(2,1)}), bf16[8,96,1024]{2,1,0:T(8,128)(2,1)S(1)}, u32[]{:S(2)}, u32[]{:S(2)}) %all-to-all-start) | async-done | bytes 1572896 | tf_op jit(solution)/shard_map/all_to_all | solution.py:18
  39.0 0.0 copy-start.2
  39.0 87.0 %gather_fusion.1 = bf16[20480,1024]{1,0:T(8,128)(2,1)} fusion(bf16[768,1024]{1,0:T(8,128)(2,1)S(1)} %bitcast.9, s32[20480]{0:T(1024)S(1)} %broadcast_clamp_fusion), kind=kCustom, calls=%fused_computation.1 | custom fusion | bytes 83968000 | tf_op jit(solution)/shard_map/jit(_take)/gather | solution.py:23
  125.9 0.0 copy-done.2
  125.9 0.0 copy-start.3
  125.9 0.0 copy-start.1
  125.9 29.3 %multiply_reduce_fusion = f32[40,512]{1,0:T(8,128)} fusion(f32[1024]{0:T(1024)S(1)} %copy-done.2, bf16[40,512,1024]{2,1,0:T(8,128)(2,1)} %bitcast.10, pred[40,512]{1,0:T(8,128)(4,1)S(1)} %get-tuple-element.2, bf16[40,512,512]{2,1,0:T(8,128)(2,1)} %param.9, pred[40,512]{1,0:T(8,128)(4,1)S(1)} %iota_compare_fusion), kind=kOutput, calls=%fused_computation.2 | convolution fusion | flops 21569187840 | bytes 63041536 | tf_op jit(solution)/shard_map/bps,bsk->bpk/dot_general | solution.py:27
  155.2 0.0 all-reduce.2.cloned.1.call-update
  155.3 33.8 %all-reduce.2.cloned.1.call-done = f32[40,512]{1,0:T(8,128)} async-done(((f32[40,512]{1,0:T(8,128)}), f32[40,512]{1,0:T(8,128)}) %all-reduce.2.cloned.1.call-update) | async-done | bytes 81936 | tf_op jit(solution)/shard_map/psum | solution.py:31
  189.0 7.9 %fusion.11 = f32[40,1,49]{2,1,0:T(1,128)S(1)} fusion(f32[40,49,512]{2,0,1:T(8,128)} %param.13, f32[40,512,1]{1,0,2:T(8,128)} %bitcast.14), kind=kOutput, calls=%fused_computation.10 | convolution fusion | flops 12042240 | bytes 4103840 | tf_op jit(solution)/shard_map/blp,bp->bl/dot_general | solution.py:32
  196.9 0.0 copy-done.3
  196.9 0.2 fusion.19
  197.2 23.0 %psum.15 = f32[64,49]{0,1:T(8,128)} all-reduce(f32[64,49]{0,1:T(8,128)S(1)} %fusion.19), channel_id=1, replica_groups=mesh['row'=8,'col'=4] {'row'}, use_global_device_ids=true, to_apply=%region_2.3 | all-reduce | flops 3136 | bytes 25088 | tf_op jit(solution)/shard_map/psum | solution.py:36
  220.2 1.3 constant_dynamic-slice_fusion
  221.5 0.0 copy-done.1
  (5 shorter events, 0.1 us)
Async XLA Ops:
  7.2 1.4 copy-start
  12.8 26.2 %all-to-all-start = ((bf16[8,96,1024]{2,1,0:T(8,128)(2,1)}), bf16[8,96,1024]{2,1,0:T(8,128)(2,1)S(1)}, u32[]{:S(2)}, u32[]{:S(2)}) async-start(bf16[8,96,1024]{2,1,0:T(8,128)(2,1)} %broadcast_select_fusion), calls=%async_computation | async-start | bytes 3145728 | tf_op jit(solution)/shard_map/all_to_all | solution.py:18
  18.0 171.1 %all-reduce.2.cloned.1.call-start = ((), (), s32[]{:S(2)}) async-start(), calls=%async_computation.1 | async-start | bytes 163840 | tf_op jit(solution)/shard_map/psum | solution.py:31
  39.0 87.0 %copy-start.2 = (f32[1024]{0:T(1024)S(1)}, f32[1024]{0:T(1024)}, u32[]{:S(2)}) copy-start(f32[1024]{0:T(1024)} %param.8) | copy-start | bytes 12292
  125.9 71.0 %copy-start.3 = (s32[40]{0:T(128)S(1)}, s32[40]{0:T(128)}, u32[]{:S(2)}) copy-start(s32[40]{0:T(128)} %param.12) | copy-start | bytes 484
  125.9 95.6 %copy-start.1 = (bf16[768,1024]{1,0:T(8,128)(2,1)S(1)}, bf16[768,1024]{1,0:T(8,128)(2,1)}, u32[]{:S(2)}) copy-start(bf16[768,1024]{1,0:T(8,128)(2,1)} %param.7) | copy-start | bytes 4718596
Sparse Core Ops, SparseCore 0:
  155.4 33.6 all-reduce.1
where the time goes:
time: 229 us; the launch traced here: 228 us
  local copies, waits for them, and re-layouts  92.3 us (40%)
  waiting for transfers between devices  52.9 us (23%)
  matrix products  37.5 us (16%)
  blocking collectives  23 us (10%)
  between operations  14.1 us (6%)
  starting transfers between devices  5.24 us (2%)
  other arithmetic  3.37 us (1%)
    gather x1, local copies, waits for them, and re-layouts, shards(): selected = jnp.take(window, local_ids, axis=0)  87 us
    psum x1, waiting for transfers between devices, shards(): full_density = lax.psum(partial_density, 'col')  33.8 us
    dot_general x1, matrix products, shards(): jnp.einsum('bps,bsk->bpk', masked, selected, preferred_element_type=jnp.f...  29.3 us
    psum x1, blocking collectives, shards(): moments = lax.psum(atom_part, 'row')  23 us
    all_to_all x1, waiting for transfers between devices, shards(): lax.all_to_all(outgoing, 'row', split_axis=0, concat_axis=0, tiled=True)  19.1 us
    dot_general x1, matrix products, shards(): jnp.einsum('blp,bp->bl', harmonics, full_density, precision=lax.Precision...  7.89 us
    all_to_all x1, starting transfers between devices, shards(): lax.all_to_all(outgoing, 'row', split_axis=0, concat_axis=0, tiled=True)  5.2 us
  transfers between devices with their start and end apart: 2, of which 2 were waited for; matrix products, arithmetic and copies ran while one was open for 1% of the time, Pallas kernels for 0%

commit v1 on v0

--- a/solution.py
+++ b/solution.py
@@ -28,7 +28,17 @@
     partial_density = jnp.sum(orbital * orbital * occupation[None, None, :], axis=2)
     atom_ids = lax.broadcasted_iota(jnp.int32, (batches, NATOM), 1)
     member = (batch_atom[:, None] == atom_ids).astype(jnp.float32)
-    full_density = lax.psum(partial_density, "col")
+
+    def _follow_cubes(inputs):
+        n_parts = lax.axis_size("col")
+        carry = inputs
+        for rr in [h for h in (1, 2, 4, 8, 16) if h < n_parts]:
+            tmp = tuple(((j0, j0 ^ rr) for j0 in range(n_parts)))
+            b_now = lax.ppermute(carry, "col", tmp)
+            carry = carry + b_now
+        return carry
+
+    full_density = _follow_cubes(partial_density)
     local_moment = jnp.einsum(
         "blp,bp->bl", harmonics, full_density, precision=lax.Precision.HIGHEST
     )

time: 229 us -> 192 us (0.84)
  waiting for transfers between devices: 52.9 us -> 27.2 us
  between operations: 14.1 us -> 0.71 us
  starting transfers between devices: 5.24 us -> 8.86 us
    psum x1 -> x0, waiting for transfers between devices: 33.8 us -> none  [shards(): full_density = lax.psum(partial_density, 'col')]
    ppermute x0 -> x2, waiting for transfers between devices: none -> 8 us  [_follow_cubes(): b_now = lax.ppermute(carry, 'col', tmp)]
    ppermute x0 -> x2, starting transfers between devices: none -> 3.67 us  [_follow_cubes(): b_now = lax.ppermute(carry, 'col', tmp)]
  transfers between devices with their start and end apart: 2 -> 3, of which waited for: 2 -> 3; matrix products, arithmetic and copies ran while one was open for 1% -> 1% of each run, Pallas kernels for 0% -> 0%
where the time goes in v1:
time: 192 us
  local copies, waits for them, and re-layouts  91.9 us (48%)
  matrix products  36.7 us (19%)
  waiting for transfers between devices  27.2 us (14%)
  blocking collectives  23 us (12%)
  starting transfers between devices  8.86 us (5%)
  other arithmetic  3.4 us (2%)
    gather x1, local copies, waits for them, and re-layouts, shards(): selected = jnp.take(window, local_ids, axis=0)  87.3 us
    dot_general x1, matrix products, shards(): jnp.einsum('bps,bsk->bpk', masked, selected, preferred_element_type=jnp.f...  28.6 us
    psum x1, blocking collectives, shards(): moments = lax.psum(atom_part, 'row')  23 us
    all_to_all x1, waiting for transfers between devices, shards(): lax.all_to_all(outgoing, 'row', split_axis=0, concat_axis=0, tiled=True)  19.2 us
    ppermute x2, waiting for transfers between devices, _follow_cubes(): b_now = lax.ppermute(carry, 'col', tmp)  8 us
    dot_general x1, matrix products, shards(): jnp.einsum('blp,bp->bl', harmonics, full_density, precision=lax.Precision...  7.84 us
    all_to_all x1, starting transfers between devices, shards(): lax.all_to_all(outgoing, 'row', split_axis=0, concat_axis=0, tiled=True)  5.2 us
  transfers between devices with their start and end apart: 3, of which 3 were waited for; matrix products, arithmetic and copies ran while one was open for 1% of the time, Pallas kernels for 0%

profile of v1, /device:TPU:0, one launch (start us, length us, event | category | flops | bytes accessed | tf_op | source)
XLA Modules:
  0.0 191.8 jit_solution(6720098487561837298)
XLA Ops:
  0.6 0.0 copy-start
  0.7 0.1 add_remainder_fusion
  0.7 0.1 compare_and_fusion.1
  0.8 0.1 rem.52
  0.9 1.1 copy-done
  2.0 2.8 %gather_fusion = bf16[768,1024]{1,0:T(8,128)(2,1)S(1)} fusion(bf16[768,1024]{1,0:T(8,128)(2,1)S(1)} %copy-done, s32[1024]{0:T(1024)S(1)} %pad_clamp_fusion), kind=kCustom, calls=%fused_computation | custom fusion | bytes 3148800 | tf_op jit(solution)/shard_map/jit(_take)/gather | solution.py:17
  4.9 1.4 broadcast_select_fusion
  6.2 5.2 %all-to-all-start = ((bf16[8,96,1024]{2,1,0:T(8,128)(2,1)}), bf16[8,96,1024]{2,1,0:T(8,128)(2,1)S(1)}, u32[]{:S(2)}, u32[]{:S(2)}) async-start(bf16[8,96,1024]{2,1,0:T(8,128)(2,1)} %broadcast_select_fusion), calls=%async_computation | async-start | bytes 3145728 | tf_op jit(solution)/shard_map/all_to_all | solution.py:18
  11.4 1.0 compare_and_fusion
  12.5 0.7 iota_compare_fusion
  13.3 19.2 %all-to-all-done = bf16[8,96,1024]{2,1,0:T(8,128)(2,1)S(1)} async-done(((bf16[8,96,1024]{2,1,0:T(8,128)(2,1)}), bf16[8,96,1024]{2,1,0:T(8,128)(2,1)S(1)}, u32[]{:S(2)}, u32[]{:S(2)}) %all-to-all-start) | async-done | bytes 1572896 | tf_op jit(solution)/shard_map/all_to_all | solution.py:18
  32.4 0.0 copy-start.2
  32.4 87.3 %gather_fusion.1 = bf16[20480,1024]{1,0:T(8,128)(2,1)} fusion(bf16[768,1024]{1,0:T(8,128)(2,1)S(1)} %bitcast.9, s32[20480]{0:T(1024)S(1)} %broadcast_clamp_fusion), kind=kCustom, calls=%fused_computation.1 | custom fusion | bytes 83968000 | tf_op jit(solution)/shard_map/jit(_take)/gather | solution.py:23
  119.7 0.0 copy-done.2
  119.7 0.0 copy-start.3
  119.7 0.0 copy-start.1
  119.7 28.6 %multiply_reduce_fusion = f32[40,512]{1,0:T(8,128)S(1)} fusion(f32[1024]{0:T(1024)S(1)} %copy-done.2, bf16[40,512,1024]{2,1,0:T(8,128)(2,1)} %bitcast.10, pred[40,512]{1,0:T(8,128)(4,1)S(1)} %get-tuple-element.2, bf16[40,512,512]{2,1,0:T(8,128)(2,1)} %param.9, pred[40,512]{1,0:T(8,128)(4,1)S(1)} %iota_compare_fusion), kind=kOutput, calls=%fused_computation.2 | convolution fusion | flops 21569187840 | bytes 63041536 | tf_op jit(solution)/shard_map/bps,bsk->bpk/dot_general | solution.py:27
  148.4 1.6 collective-permute-start
  150.0 3.7 %collective-permute-done = f32[40,512]{1,0:T(8,128)S(1)} collective-permute-done((f32[40,512]{1,0:T(8,128)S(1)}, f32[40,512]{1,0:T(8,128)S(1)}, u32[]{:S(2)}, u32[]{:S(2)}) %collective-permute-start) | collective-permute-done | bytes 81952 | tf_op jit(solution)/shard_map/ppermute | solution.py:37
  153.8 2.0 %collective-permute-start.1 = (f32[40,512]{1,0:T(8,128)S(1)}, f32[40,512]{1,0:T(8,128)S(1)}, u32[]{:S(2)}, u32[]{:S(2)}) collective-permute-start(f32[40,512]{1,0:T(8,128)S(1)} %add.99), channel_id=1, source_target_pairs={{0,2},{1,3},{2,0},{3,1},{4,6},{5,7},{6,4},{7,5},{8,10},{9,11},{10,... | collective-permute-start | bytes 245768 | tf_op jit(solution)/shard_map/ppermute | solution.py:37
  155.8 4.3 %collective-permute-done.1 = f32[40,512]{1,0:T(8,128)S(1)} collective-permute-done((f32[40,512]{1,0:T(8,128)S(1)}, f32[40,512]{1,0:T(8,128)S(1)}, u32[]{:S(2)}, u32[]{:S(2)}) %collective-permute-start.1) | collective-permute-done | bytes 81952 | tf_op jit(solution)/shard_map/ppermute | solution.py:37
  160.1 7.8 %fusion.11 = f32[40,1,49]{2,1,0:T(1,128)S(1)} fusion(f32[40,49,512]{2,0,1:T(8,128)} %param.13, f32[40,512,1]{1,0,2:T(8,128)S(1)} %bitcast.12), kind=kOutput, calls=%fused_computation.10 | convolution fusion | flops 12042240 | bytes 4103840 | tf_op jit(solution)/shard_map/blp,bp->bl/dot_general | solution.py:42
  167.9 0.0 copy-done.3
  167.9 0.2 fusion.19
  168.2 23.0 %psum.7 = f32[64,49]{0,1:T(8,128)} all-reduce(f32[64,49]{0,1:T(8,128)S(1)} %fusion.19), channel_id=1, replica_groups=mesh['row'=8,'col'=4] {'row'}, use_global_device_ids=true, to_apply=%region_1.2 | all-reduce | flops 3136 | bytes 25088 | tf_op jit(solution)/shard_map/psum | solution.py:46
  191.1 0.6 constant_dynamic-slice_fusion
  191.8 0.0 copy-done.1
  (7 shorter events, 0.1 us)
Async XLA Ops:
  0.6 1.4 copy-start
  6.2 26.2 %all-to-all-start = ((bf16[8,96,1024]{2,1,0:T(8,128)(2,1)}), bf16[8,96,1024]{2,1,0:T(8,128)(2,1)S(1)}, u32[]{:S(2)}, u32[]{:S(2)}) async-start(bf16[8,96,1024]{2,1,0:T(8,128)(2,1)} %broadcast_select_fusion), calls=%async_computation | async-start | bytes 3145728 | tf_op jit(solution)/shard_map/all_to_all | solution.py:18
  32.4 87.3 %copy-start.2 = (f32[1024]{0:T(1024)S(1)}, f32[1024]{0:T(1024)}, u32[]{:S(2)}) copy-start(f32[1024]{0:T(1024)} %param.8) | copy-start | bytes 12292
  119.7 48.2 %copy-start.3 = (s32[40]{0:T(128)S(1)}, s32[40]{0:T(128)}, u32[]{:S(2)}) copy-start(s32[40]{0:T(128)} %param.12) | copy-start | bytes 484
  119.7 72.1 %copy-start.1 = (bf16[768,1024]{1,0:T(8,128)(2,1)S(1)}, bf16[768,1024]{1,0:T(8,128)(2,1)}, u32[]{:S(2)}) copy-start(bf16[768,1024]{1,0:T(8,128)(2,1)} %param.7) | copy-start | bytes 4718596
  148.4 5.4 %collective-permute-start = (f32[40,512]{1,0:T(8,128)S(1)}, f32[40,512]{1,0:T(8,128)S(1)}, u32[]{:S(2)}, u32[]{:S(2)}) collective-permute-start(f32[40,512]{1,0:T(8,128)S(1)} %multiply_reduce_fusion), channel_id=1, source_target_pairs={{0,1},{1,0},{2,3},{3,2},{4,5},{5,4},{6,7},{7,6},{8,9},{9,8},{10,11... | collective-permute-start | bytes 245768 | tf_op jit(solution)/shard_map/ppermute | solution.py:37
  153.8 6.3 %collective-permute-start.1 = (f32[40,512]{1,0:T(8,128)S(1)}, f32[40,512]{1,0:T(8,128)S(1)}, u32[]{:S(2)}, u32[]{:S(2)}) collective-permute-start(f32[40,512]{1,0:T(8,128)S(1)} %add.99), channel_id=1, source_target_pairs={{0,2},{1,3},{2,0},{3,1},{4,6},{5,7},{6,4},{7,5},{8,10},{9,11},{10,... | collective-permute-start | bytes 245768 | tf_op jit(solution)/shard_map/ppermute | solution.py:37
